TPU v7x, 32 devices: a whole 2x2x4 slice. The times are simulated.
32 devices in a mesh: batch: 4 (over x, core), centers: 8 (over z, y).
Axes of the slice: x: 2, y: 2, z: 4, core: 2. Of those that a mesh axis runs over, the one named last changes fastest.
Arguments:
- pool_features: float32 [32768, 128], P(('batch', 'centers')), may hold values from -14 to 14
- pool_targets: float32 [32768, 64], P(('batch', 'centers')), may hold values from -6 to 6
- batch_index: int32 [2048], P(('batch', 'centers')), may hold values from 0 to 1023
- centers: float32 [4096, 128], P('centers'), may hold values from -14 to 14
- weights: float32 [4096, 64], P('centers'), as said below
- eig_vectors: float32 [4096, 1024], P(('batch', 'centers')), may hold values from -0.09375 to 0.09375
- eig_scale: float32 [1024], replicated, may hold values from 0.5 to 4
- nys_owner: int32 [4096, 1], P(('batch', 'centers')), may hold values from 0 to 7; in each aligned block of 128 rows (0 to 127, 128 to 255, ...) at most 32 rows name the same one
- nys_offset: int32 [4096], P(('batch', 'centers')), may hold values from 0 to 511
Outputs:
- residual_out: float32 [2048, 64], P(('batch', 'centers'))
- update: float32 [4096, 64], P('centers')
Inputs may be any that keep to these rules, and one draw needn't show every extreme that they name: `nys_owner`: among the 128 rows of one device no owner is named more than 32 times; on some devices one owner is named exactly 32 times. `weights`: every column sums to zero.
All inputs are finite; a program needn't handle non-finite values.
Results may differ from a plain program's by a relative error of at most 0.0003.
Values sent between devices are 32-bit elements; how exact they have to be, the bound alone decides.
A program may use at most 64 MiB of HBM per device.

v0:
```python
import math
import jax
import jax.numpy as jnp
from jax import lax
from jax.sharding import PartitionSpec as P

DEPTH = 3
epsilon = 1e-06
highest = lax.Precision.HIGHEST


def kernel_rows(row_block, center_block, center_norm):
    inner_prod = (
        lax.dot_general(
            row_block,
            center_block,
            (((1,), (1,)), ((), ())),
            precision=highest,
            preferred_element_type=jnp.float32,
        )
        / row_block.shape[1]
    )
    row_norm = jnp.mean(row_block * row_block, axis=1) + epsilon
    norm_scale = jnp.sqrt(row_norm[:, None] * center_norm[None, :])
    sigma_now = inner_prod
    tangent = inner_prod
    for depth_step in range(DEPTH):
        cosine = sigma_now / norm_scale
        arc_angle = jnp.arccos(cosine)
        remain = (math.pi - arc_angle) / math.pi
        sigma_now = (
            norm_scale
            * (jnp.sqrt(1.0 - cosine * cosine) + (math.pi - arc_angle) * cosine)
            / math.pi
        )
        tangent = sigma_now + tangent * remain
    return tangent


def per_device(
    pool_features,
    pool_targets,
    batch_index,
    centers,
    weights,
    eig_vectors,
    eig_scale,
    nys_owner,
    nys_offset,
):
    local_rows = pool_features[batch_index]
    local_targets = pool_targets[batch_index]
    row_count = local_rows.shape[0]
    group_size = lax.axis_size("centers")
    rows_total = row_count * group_size * lax.axis_size("batch")
    center_count = centers.shape[0]
    outputs = weights.shape[1]
    center_norm = jnp.mean(centers * centers, axis=1) + epsilon
    kernel = kernel_rows(
        lax.all_gather(local_rows, "centers", axis=0, tiled=True), centers, center_norm
    )
    partial_pred = jnp.dot(kernel, weights, precision=highest, preferred_element_type=jnp.float32)
    all_targets = lax.all_gather(local_targets, "centers", axis=0, tiled=True)
    prediction = lax.psum(partial_pred, "centers")
    residual = prediction - all_targets
    own_residual = lax.dynamic_slice_in_dim(
        residual, lax.axis_index("centers") * row_count, row_count, 0
    )
    grads_part = lax.dot_general(
        kernel,
        residual,
        (((0,), (0,)), ((), ())),
        precision=highest,
        preferred_element_type=jnp.float32,
    ) / math.sqrt(rows_total)
    grads = lax.psum(grads_part, "batch")
    owner = nys_owner[:, 0]
    slots = max(2, 2 * owner.shape[0] // group_size)
    owner_hot = (owner[:, None] == jnp.arange(group_size, dtype=jnp.int32)[None, :]).astype(
        jnp.int32
    )
    slot_rank = jnp.sum((jnp.cumsum(owner_hot, axis=0) - owner_hot) * owner_hot, axis=1)
    requests = jnp.zeros((group_size, slots), jnp.int32).at[owner, slot_rank].set(nys_offset)
    received = lax.all_to_all(requests, "centers", split_axis=0, concat_axis=0, tiled=True)
    found = grads[received]
    returned = lax.all_to_all(found, "centers", split_axis=0, concat_axis=0, tiled=True)
    picked_grads = returned[owner, slot_rank]
    coeff_part = lax.dot_general(
        eig_vectors,
        picked_grads,
        (((0,), (0,)), ((), ())),
        precision=highest,
        preferred_element_type=jnp.float32,
    )
    coeff = lax.psum(coeff_part, ("batch", "centers"))
    corr_rows = jnp.dot(
        eig_vectors,
        eig_scale[:, None] * coeff,
        precision=highest,
        preferred_element_type=jnp.float32,
    )
    outgoing = (
        jnp.zeros((group_size, slots, outputs), jnp.float32).at[owner, slot_rank].set(corr_rows)
    )
    incoming = lax.all_to_all(outgoing, "centers", split_axis=0, concat_axis=0, tiled=True)
    corr_part = jnp.zeros((center_count, outputs), jnp.float32).at[received].add(incoming)
    correction = lax.psum(corr_part, "batch")
    return (own_residual, correction - grads)


def solution(mesh):
    placed = (
        P(("batch", "centers"), None),
        P(("batch", "centers"), None),
        P(("batch", "centers")),
        P("centers", None),
        P("centers", None),
        P(("batch", "centers"), None),
        P(),
        P(("batch", "centers"), None),
        P(("batch", "centers")),
    )
    return jax.shard_map(
        per_device,
        mesh=mesh,
        in_specs=placed,
        out_specs=(P(("batch", "centers"), None), P("centers", None)),
        check_vma=False,
    )
```

profile of v0, /device:TPU:0, one launch (start us, length us, event | category | flops | bytes accessed | tf_op | source)
XLA Modules:
  0.0 387.0 jit_solution(5106888059048131326)
XLA Ops:
  7.2 0.0 copy-start
  7.2 0.0 copy-start.6
  7.2 0.7 copy-done.6
  7.9 0.1 fusion.4
  8.0 0.2 reduce_window_sum.11
  8.2 0.2 select_reduce_fusion
  8.3 0.0 copy-start.8
  8.4 0.6 broadcast.104
  9.0 0.1 copy-done.8
  9.0 19.9 %scatter_fusion = s32[8,32]{1,0:T(8,128)} fusion(s32[8,32]{1,0:T(8,128)} %broadcast.104, s32[128]{0:T(128)S(1)} %get-tuple-element.8, s32[128]{0:T(128)S(1)} %copy-done.8), kind=kCustom, calls=%fused_computation.4 | custom fusion | bytes 2560 | tf_op jit(solution)/shard_map/scatter | solution.py:83
  28.9 7.4 %all-to-all-start = ((s32[8,1,32]{2,1,0:T(1,128)}), s32[8,1,32]{2,1,0:T(1,128)S(1)}, u32[]{:S(2)}, u32[]{:S(2)}) async-start(s32[8,1,32]{2,1,0:T(1,128)} %bitcast.4), calls=%async_computation | async-start | bytes 8192 | tf_op jit(solution)/shard_map/all_to_all | solution.py:84
  36.3 0.0 all-reduce.5.cloned.1.call-start
  36.4 0.0 copy-done.9
  36.4 0.1 multiply_reduce_fusion
  36.6 0.6 gather_fusion
  37.2 31.2 %all-gather = f32[512,128]{1,0:T(8,128)S(1)} all-gather(f32[64,128]{1,0:T(8,128)S(1)} %gather_fusion), channel_id=2, replica_groups=mesh['batch'=4,'centers'=8] {'centers'}, dimensions={0}, use_global_device_ids=true | all-gather | bytes 294912 | tf_op jit(solution)/shard_map/all_gather | solution.py:60
  68.4 0.1 multiply_reduce_fusion.1
  68.6 0.0 copy-start.4
  68.6 8.9 %multiply_add_fusion = f32[512,512]{1,0:T(8,128)S(1)} fusion(f32[512,128]{1,0:T(8,128)S(1)} %all-gather, f32[512,128]{1,0:T(8,128)S(1)} %copy-done.3, f32[512]{0:T(512)S(1)} %multiply_add_fusion.1, f32[512]{0:T(512)S(1)} %multiply_add_fusion.2), kind=kOutput, calls=%fused_computation.11 | convolution fusion | flops 414187520 | bytes 1576960 | tf_op jit(solution)/shard_map/dot_general | solution.py:14
  77.5 0.0 copy-start.2
  77.5 1.8 fusion.8
  79.3 0.0 all-reduce.5.cloned.1.call-update
  79.4 0.0 all-reduce.7.cloned.1.call-start
  79.4 0.2 copy.23
  79.6 0.6 gather_fusion.1
  80.2 30.8 %all-gather.1 = f32[512,64]{1,0:T(8,128)S(1)} all-gather(f32[64,64]{1,0:T(8,128)S(1)} %gather_fusion.1), channel_id=3, replica_groups=mesh['batch'=4,'centers'=8] {'centers'}, dimensions={0}, use_global_device_ids=true | all-gather | bytes 147456 | tf_op jit(solution)/shard_map/all_gather | solution.py:63
  111.1 0.1 copy.24
  111.2 0.0 all-to-all-done
  111.2 0.1 reshape.100
  111.3 39.5 %all-reduce.5.cloned.1.call-done = f32[512,64]{0,1:T(8,128)} async-done(((f32[512,64]{0,1:T(8,128)}), f32[512,64]{0,1:T(8,128)}) %all-reduce.5.cloned.1.call-update) | async-done | bytes 131088 | tf_op jit(solution)/shard_map/psum | solution.py:64
  150.8 0.9 sub.36
  151.7 1.5 convolution_multiply_fusion.1
  153.2 0.0 all-reduce.7.cloned.1.call-update
  153.2 0.0 all-reduce.9.cloned.1.call-start
  153.3 31.3 %all-reduce.7.cloned.1.call-done = f32[512,64]{0,1:T(8,128)} async-done(((f32[512,64]{0,1:T(8,128)}), f32[512,64]{0,1:T(8,128)}) %all-reduce.7.cloned.1.call-update) | async-done | bytes 131088 | tf_op jit(solution)/shard_map/psum | solution.py:76
  184.6 1.0 copy.26
  185.6 0.7 gather_fusion.2
  186.3 0.1 reshape.114
  186.5 12.2 %all_to_all.22 = f32[8,1,2048]{2,1,0:T(1,128)S(1)} all-to-all(f32[8,1,2048]{2,1,0:T(1,128)S(1)} %reshape.114), channel_id=1, replica_groups=mesh['batch'=4,'centers'=8] {'centers'}, dimensions={0} | all-to-all | bytes 131072 | tf_op jit(solution)/shard_map/all_to_all | solution.py:86
  198.7 0.5 broadcast.212
  199.2 0.8 reduce
  200.0 0.1 reshape.115
  200.1 1.2 gather_fusion.3
  201.3 0.0 copy-done
  201.3 1.1 convolution_bitcast_fusion
  202.5 0.0 all-reduce.9.cloned.1.call-update
  202.5 123.4 %all-reduce.9.cloned.1.call-done = f32[1024,64]{0,1:T(8,128)} async-done(((f32[1024,64]{0,1:T(8,128)}), f32[1024,64]{0,1:T(8,128)}) %all-reduce.9.cloned.1.call-update) | async-done | bytes 262160 | tf_op jit(solution)/shard_map/psum | solution.py:95
  325.9 1.6 convolution_bitcast_fusion.1
  327.5 0.1 copy.27
  327.7 6.9 %scatter_fusion.1 = f32[8,32,64]{2,1,0:T(8,128)S(1)} fusion(f32[8,32,64]{2,1,0:T(8,128)S(1)} %broadcast_in_dim.8, s32[128]{0:T(128)S(1)} %get-tuple-element.8, f32[128,64]{1,0:T(8,128)S(1)} %copy.27), kind=kCustom, calls=%fused_computation.5 | custom fusion | bytes 99328 | tf_op jit(solution)/shard_map/scatter | solution.py:103
  334.6 0.8 reshape.116
  335.3 4.5 %all-to-all-start.2 = ((f32[8,1,2048]{2,1,0:T(1,128)}), f32[8,1,2048]{2,1,0:T(1,128)S(1)}, u32[]{:S(2)}, u32[]{:S(2)}) async-start(f32[8,1,2048]{2,1,0:T(1,128)} %reshape.116), calls=%async_computation.2 | async-start | bytes 131072 | tf_op jit(solution)/shard_map/all_to_all | solution.py:105
  339.8 0.0 all-reduce.11.cloned.1.call-start
  339.9 6.9 %all-to-all-done.2 = f32[8,1,2048]{2,1,0:T(1,128)S(1)} async-done(((f32[8,1,2048]{2,1,0:T(1,128)}), f32[8,1,2048]{2,1,0:T(1,128)S(1)}, u32[]{:S(2)}, u32[]{:S(2)}) %all-to-all-start.2) | async-done | bytes 65568 | tf_op jit(solution)/shard_map/all_to_all | solution.py:105
  346.7 0.8 reduce.1
  347.6 0.1 reshape.117
  347.6 1.7 scatter_custom_fusion.2
  349.4 0.8 copy.28
  350.2 0.0 all-reduce.11.cloned.1.call-update
  350.2 0.1 constant_dynamic-slice_fusion
  350.3 0.7 copy.29
  351.0 27.9 %all-reduce.11.cloned.1.call-done = f32[512,64]{0,1:T(8,128)} async-done(((f32[512,64]{0,1:T(8,128)}), f32[512,64]{0,1:T(8,128)}) %all-reduce.11.cloned.1.call-update) | async-done | bytes 131088 | tf_op jit(solution)/shard_map/psum | solution.py:107
  378.9 0.0 copy-done.1
  378.9 1.6 sub.38
  (18 shorter events, 0.1 us)
Async XLA Ops:
  7.2 194.2 %copy-start = (f32[128,1024]{1,0:T(8,128)S(1)}, f32[128,1024]{1,0:T(8,128)}, u32[]{:S(2)}) copy-start(f32[128,1024]{1,0:T(8,128)} %param.14) | copy-start | bytes 1572868
  7.2 0.7 copy-start.6
  8.3 0.7 copy-start.8
  9.0 27.4 %copy-start.3 = (f32[512,128]{1,0:T(8,128)S(1)}, f32[512,128]{1,0:T(8,128)}, u32[]{:S(2)}) copy-start(f32[512,128]{1,0:T(8,128)} %param.12) | copy-start | bytes 786436
  9.0 27.6 %copy-start.5 = (f32[1024,128]{1,0:T(8,128)S(1)}, f32[1024,128]{1,0:T(8,128)}, u32[]{:S(2)}) copy-start(f32[1024,128]{1,0:T(8,128)} %param.9) | copy-start | bytes 1572868
  28.9 7.5 %copy-start.9 = (s32[64]{0:T(128)S(1)}, s32[64]{0:T(128)}, u32[]{:S(2)}) copy-start(s32[64]{0:T(128)} %param.11) | copy-start | bytes 772
  28.9 82.3 %all-to-all-start = ((s32[8,1,32]{2,1,0:T(1,128)}), s32[8,1,32]{2,1,0:T(1,128)S(1)}, u32[]{:S(2)}, u32[]{:S(2)}) async-start(s32[8,1,32]{2,1,0:T(1,128)} %bitcast.4), calls=%async_computation | async-start | bytes 8192 | tf_op jit(solution)/shard_map/all_to_all | solution.py:84
  36.3 114.5 %all-reduce.5.cloned.1.call-start = ((), (), s32[]{:S(2)}) async-start(), calls=%async_computation.3 | async-start | bytes 262144 | tf_op jit(solution)/shard_map/psum | solution.py:64
  68.6 8.9 %copy-start.4 = (f32[512,64]{0,1:T(8,128)S(1)}, f32[512,64]{0,1:T(8,128)}, u32[]{:S(2)}) copy-start(f32[512,64]{0,1:T(8,128)} %param.13) | copy-start | bytes 393220
  77.5 1.9 copy-start.2
  79.4 105.2 %all-reduce.7.cloned.1.call-start = ((), (), s32[]{:S(2)}) async-start(), calls=%async_computation.4 | async-start | bytes 262144 | tf_op jit(solution)/shard_map/psum | solution.py:76
  153.2 172.7 %all-reduce.9.cloned.1.call-start = ((), (), s32[]{:S(2)}) async-start(), calls=%async_computation.5 | async-start | bytes 524288 | tf_op jit(solution)/shard_map/psum | solution.py:95
  202.5 123.4 %copy-start.7 = (f32[1024]{0:T(1024)S(1)}, f32[1024]{0:T(1024)}, u32[]{:S(2)}) copy-start(f32[1024]{0:T(1024)} %param.15) | copy-start | bytes 12292
  335.3 11.4 %all-to-all-start.2 = ((f32[8,1,2048]{2,1,0:T(1,128)}), f32[8,1,2048]{2,1,0:T(1,128)S(1)}, u32[]{:S(2)}, u32[]{:S(2)}) async-start(f32[8,1,2048]{2,1,0:T(1,128)} %reshape.116), calls=%async_computation.2 | async-start | bytes 131072 | tf_op jit(solution)/shard_map/all_to_all | solution.py:105
  339.8 39.0 %all-reduce.11.cloned.1.call-start = ((), (), s32[]{:S(2)}) async-start(), calls=%async_computation.6 | async-start | bytes 262144 | tf_op jit(solution)/shard_map/psum | solution.py:107
  350.1 28.7 %copy-start.1 = (f32[512,64]{0,1:T(8,128)S(1)}, f32[512,64]{0,1:T(8,128)}, u32[]{:S(2)}) copy-start(f32[512,64]{0,1:T(8,128)} %all-reduce.7.cloned.1.call-done) | copy-start | bytes 393220
Sparse Core Ops, SparseCore 0:
  79.5 71.2 all-reduce.4
  153.7 30.8 all-reduce.6
  202.6 123.2 all-reduce.8
  350.3 28.5 all-reduce.10
where the time goes:
time: 388 us; the launch traced here: 387 us
  waiting for transfers between devices  229 us (59%)
  blocking collectives  74.3 us (19%)
  local copies, waits for them, and re-layouts  36 us (9%)
  matrix products  14.9 us (4%)
  between operations  14 us (4%)
  starting transfers between devices  12.1 us (3%)
  other arithmetic  6.6 us (2%)
    psum x1, waiting for transfers between devices, per_device(): coeff = lax.psum(coeff_part, ('batch', 'centers'))  123 us
    psum x1, waiting for transfers between devices, per_device(): prediction = lax.psum(partial_pred, 'centers')  39.5 us
    psum x1, waiting for transfers between devices, per_device(): grads = lax.psum(grads_part, 'batch')  31.3 us
    all_gather x1, blocking collectives, per_device(): lax.all_gather(local_rows, 'centers', axis=0, tiled=True)  31.2 us
    all_gather x1, blocking collectives, per_device(): all_targets = lax.all_gather(local_targets, 'centers', axis=0, tiled=True)  30.8 us
    psum x1, waiting for transfers between devices, per_device(): correction = lax.psum(corr_part, 'batch')  27.9 us
    scatter x1, local copies, waits for them, and re-layouts, per_device(): jnp.zeros((group_size, slots), jnp.int32).at[owner, slot_rank]  19.9 us
    all_to_all x1, blocking collectives, per_device(): lax.all_to_all(found, 'centers', split_axis=0, concat_axis=0, tiled=True)  12.2 us
  transfers between devices with their start and end apart: 6, of which 5 were waited for; matrix products, arithmetic and copies ran while one was open for 3% of the time, Pallas kernels for 0%

commit v1 on v0

--- a/solution.py
+++ b/solution.py
@@ -104,7 +104,11 @@
     )
     incoming = lax.all_to_all(outgoing, "centers", split_axis=0, concat_axis=0, tiled=True)
     corr_part = jnp.zeros((center_count, outputs), jnp.float32).at[received].add(incoming)
-    correction = lax.psum(corr_part, "batch")
+    correction = corr_part
+    for hop in (1, 2):
+        correction = correction + lax.ppermute(
+            correction, "batch", [(dev, dev ^ hop) for dev in range(4)]
+        )
     return (own_residual, correction - grads)
 
 

time: 388 us -> 364 us (0.938)
  waiting for transfers between devices: 229 us -> 200 us
  blocking collectives: 74.3 us -> 85.5 us
    psum x1 -> x0, waiting for transfers between devices: 27.9 us -> none  [per_device(): correction = lax.psum(corr_part, 'batch')]
    all_to_all x0 -> x1, blocking collectives: none -> 11.2 us  [per_device(): lax.all_to_all(outgoing, 'centers', split_axis=0, concat_axis=0, tiled=True)]
    all_to_all x1 -> x0, waiting for transfers between devices: 6.86 us -> none  [per_device(): lax.all_to_all(outgoing, 'centers', split_axis=0, concat_axis=0, tiled=True)]
    ppermute x0 -> x2, waiting for transfers between devices: none -> 5.48 us  [per_device(): lax.ppermute(correction, 'batch', [(dev, dev ^ hop) for dev in range(4)])]
    all_to_all x1 -> x0, starting transfers between devices: 4.52 us -> none  [per_device(): lax.all_to_all(outgoing, 'centers', split_axis=0, concat_axis=0, tiled=True)]
  transfers between devices with their start and end apart: 6 -> 6, of which waited for: 5 -> 5; matrix products, arithmetic and copies ran while one was open for 3% -> 4% of each run, Pallas kernels for 0% -> 0%
where the time goes in v1:
time: 364 us; the launch traced here: 363 us
  waiting for transfers between devices  200 us (55%)
  blocking collectives  85.5 us (23%)
  local copies, waits for them, and re-layouts  34.7 us (10%)
  matrix products  14.9 us (4%)
  between operations  14 us (4%)
  starting transfers between devices  8.32 us (2%)
  other arithmetic  5.72 us (2%)
    psum x1, waiting for transfers between devices, per_device(): coeff = lax.psum(coeff_part, ('batch', 'centers'))  123 us
    psum x1, waiting for transfers between devices, per_device(): prediction = lax.psum(partial_pred, 'centers')  39.5 us
    psum x1, waiting for transfers between devices, per_device(): grads = lax.psum(grads_part, 'batch')  31.3 us
    all_gather x1, blocking collectives, per_device(): lax.all_gather(local_rows, 'centers', axis=0, tiled=True)  31.2 us
    all_gather x1, blocking collectives, per_device(): all_targets = lax.all_gather(local_targets, 'centers', axis=0, tiled=True)  30.8 us
    scatter x1, local copies, waits for them, and re-layouts, per_device(): jnp.zeros((group_size, slots), jnp.int32).at[owner, slot_rank]  19.9 us
    all_to_all x1, blocking collectives, per_device(): lax.all_to_all(found, 'centers', split_axis=0, concat_axis=0, tiled=True)  12.2 us
    all_to_all x1, blocking collectives, per_device(): lax.all_to_all(outgoing, 'centers', split_axis=0, concat_axis=0, tiled=True)  11.2 us
  transfers between devices with their start and end apart: 6, of which 5 were waited for; matrix products, arithmetic and copies ran while one was open for 4% of the time, Pallas kernels for 0%

profile of v1, /device:TPU:0, one launch (start us, length us, event | category | flops | bytes accessed | tf_op | source)
XLA Modules:
  0.0 362.9 jit_solution(18172965295878565667)
XLA Ops:
  7.2 0.0 copy-start
  7.2 0.0 copy-start.6
  7.2 0.7 copy-done.6
  7.9 0.1 fusion.4
  8.0 0.2 reduce_window_sum.11
  8.2 0.2 select_reduce_fusion
  8.3 0.0 copy-start.8
  8.4 0.6 broadcast.104
  9.0 0.1 copy-done.8
  9.0 19.9 %scatter_fusion = s32[8,32]{1,0:T(8,128)} fusion(s32[8,32]{1,0:T(8,128)} %broadcast.104, s32[128]{0:T(128)S(1)} %get-tuple-element.8, s32[128]{0:T(128)S(1)} %copy-done.8), kind=kCustom, calls=%fused_computation.4 | custom fusion | bytes 2560 | tf_op jit(solution)/shard_map/scatter | solution.py:83
  28.9 7.4 %all-to-all-start = ((s32[8,1,32]{2,1,0:T(1,128)}), s32[8,1,32]{2,1,0:T(1,128)S(1)}, u32[]{:S(2)}, u32[]{:S(2)}) async-start(s32[8,1,32]{2,1,0:T(1,128)} %bitcast.4), calls=%async_computation | async-start | bytes 8192 | tf_op jit(solution)/shard_map/all_to_all | solution.py:84
  36.3 0.0 all-reduce.4.cloned.1.call-start
  36.4 0.0 copy-done.9
  36.4 0.1 multiply_reduce_fusion
  36.6 0.6 gather_fusion
  37.2 31.2 %all-gather = f32[512,128]{1,0:T(8,128)S(1)} all-gather(f32[64,128]{1,0:T(8,128)S(1)} %gather_fusion), channel_id=2, replica_groups=mesh['batch'=4,'centers'=8] {'centers'}, dimensions={0}, use_global_device_ids=true | all-gather | bytes 294912 | tf_op jit(solution)/shard_map/all_gather | solution.py:60
  68.4 0.1 multiply_reduce_fusion.1
  68.6 0.0 copy-start.4
  68.6 8.9 %multiply_add_fusion = f32[512,512]{1,0:T(8,128)S(1)} fusion(f32[512,128]{1,0:T(8,128)S(1)} %all-gather, f32[512,128]{1,0:T(8,128)S(1)} %copy-done.3, f32[512]{0:T(512)S(1)} %multiply_add_fusion.1, f32[512]{0:T(512)S(1)} %multiply_add_fusion.2), kind=kOutput, calls=%fused_computation.11 | convolution fusion | flops 414187520 | bytes 1576960 | tf_op jit(solution)/shard_map/dot_general | solution.py:14
  77.5 0.0 copy-done.4
  77.5 0.0 copy-start.2
  77.6 1.8 fusion.8
  79.3 0.0 all-reduce.4.cloned.1.call-update
  79.4 0.0 all-reduce.6.cloned.1.call-start
  79.4 0.2 copy.24
  79.6 0.6 gather_fusion.1
  80.2 30.8 %all-gather.1 = f32[512,64]{1,0:T(8,128)S(1)} all-gather(f32[64,64]{1,0:T(8,128)S(1)} %gather_fusion.1), channel_id=3, replica_groups=mesh['batch'=4,'centers'=8] {'centers'}, dimensions={0}, use_global_device_ids=true | all-gather | bytes 147456 | tf_op jit(solution)/shard_map/all_gather | solution.py:63
  111.1 0.1 copy.25
  111.2 0.0 all-to-all-done
  111.2 0.1 reshape.100
  111.3 39.5 %all-reduce.4.cloned.1.call-done = f32[512,64]{0,1:T(8,128)} async-done(((f32[512,64]{0,1:T(8,128)}), f32[512,64]{0,1:T(8,128)}) %all-reduce.4.cloned.1.call-update) | async-done | bytes 131088 | tf_op jit(solution)/shard_map/psum | solution.py:64
  150.8 0.9 sub.36
  151.7 1.4 convolution_multiply_fusion.1
  153.2 0.0 all-reduce.6.cloned.1.call-update
  153.2 0.0 all-reduce.8.cloned.1.call-start
  153.3 31.3 %all-reduce.6.cloned.1.call-done = f32[512,64]{0,1:T(8,128)} async-done(((f32[512,64]{0,1:T(8,128)}), f32[512,64]{0,1:T(8,128)}) %all-reduce.6.cloned.1.call-update) | async-done | bytes 131088 | tf_op jit(solution)/shard_map/psum | solution.py:76
  184.6 1.0 copy.27
  185.6 0.7 gather_fusion.2
  186.3 0.1 reshape.114
  186.5 12.2 %all_to_all.22 = f32[8,1,2048]{2,1,0:T(1,128)S(1)} all-to-all(f32[8,1,2048]{2,1,0:T(1,128)S(1)} %reshape.114), channel_id=1, replica_groups=mesh['batch'=4,'centers'=8] {'centers'}, dimensions={0} | all-to-all | bytes 131072 | tf_op jit(solution)/shard_map/all_to_all | solution.py:86
  198.7 0.5 broadcast.212
  199.2 0.8 reduce
  200.0 0.1 reshape.115
  200.1 1.2 gather_fusion.3
  201.3 1.1 convolution_bitcast_fusion
  202.5 0.0 all-reduce.8.cloned.1.call-update
  202.5 123.4 %all-reduce.8.cloned.1.call-done = f32[1024,64]{0,1:T(8,128)} async-done(((f32[1024,64]{0,1:T(8,128)}), f32[1024,64]{0,1:T(8,128)}) %all-reduce.8.cloned.1.call-update) | async-done | bytes 262160 | tf_op jit(solution)/shard_map/psum | solution.py:95
  325.9 0.0 copy-done.7
  325.9 1.6 convolution_bitcast_fusion.1
  327.5 0.1 copy.28
  327.6 6.9 %scatter_fusion.1 = f32[8,32,64]{2,1,0:T(8,128)S(1)} fusion(f32[8,32,64]{2,1,0:T(8,128)S(1)} %broadcast_in_dim.8, s32[128]{0:T(128)S(1)} %get-tuple-element.8, f32[128,64]{1,0:T(8,128)S(1)} %copy.28), kind=kCustom, calls=%fused_computation.5 | custom fusion | bytes 99328 | tf_op jit(solution)/shard_map/scatter | solution.py:103
  334.6 0.1 reshape.116
  334.7 11.2 %all_to_all.23 = f32[8,1,2048]{2,1,0:T(1,128)S(1)} all-to-all(f32[8,1,2048]{2,1,0:T(1,128)S(1)} %reshape.116), channel_id=1, replica_groups=mesh['batch'=4,'centers'=8] {'centers'}, dimensions={0} | all-to-all | bytes 131072 | tf_op jit(solution)/shard_map/all_to_all | solution.py:105
  345.9 0.8 reduce.1
  346.7 0.1 reshape.117
  346.8 1.7 scatter_custom_fusion.2
  348.5 0.1 copy.30
  348.7 0.1 collective-permute-start
  348.7 1.3 collective-permute-done
  350.1 0.7 collective-permute-start.1
  350.8 0.1 constant_dynamic-slice_fusion
  350.9 0.7 copy.31
  351.6 4.1 %collective-permute-done.1 = f32[512,64]{0,1:T(8,128)S(1)} collective-permute-done((f32[512,64]{0,1:T(8,128)S(1)}, f32[512,64]{0,1:T(8,128)S(1)}, u32[]{:S(2)}, u32[]{:S(2)}) %collective-permute-start.1) | collective-permute-done | bytes 131104 | tf_op jit(solution)/shard_map/ppermute | solution.py:109
  355.7 0.7 add_subtract_fusion
  (19 shorter events, 0.1 us)
Async XLA Ops:
  7.2 194.2 %copy-start = (f32[128,1024]{1,0:T(8,128)S(1)}, f32[128,1024]{1,0:T(8,128)}, u32[]{:S(2)}) copy-start(f32[128,1024]{1,0:T(8,128)} %param.14) | copy-start | bytes 1572868
  7.2 0.7 copy-start.6
  8.3 0.7 copy-start.8
  9.0 27.4 %copy-start.3 = (f32[512,128]{1,0:T(8,128)S(1)}, f32[512,128]{1,0:T(8,128)}, u32[]{:S(2)}) copy-start(f32[512,128]{1,0:T(8,128)} %param.12) | copy-start | bytes 786436
  9.0 27.6 %copy-start.5 = (f32[1024,128]{1,0:T(8,128)S(1)}, f32[1024,128]{1,0:T(8,128)}, u32[]{:S(2)}) copy-start(f32[1024,128]{1,0:T(8,128)} %param.9) | copy-start | bytes 1572868
  28.9 7.5 %copy-start.9 = (s32[64]{0:T(128)S(1)}, s32[64]{0:T(128)}, u32[]{:S(2)}) copy-start(s32[64]{0:T(128)} %param.11) | copy-start | bytes 772
  28.9 82.3 %all-to-all-start = ((s32[8,1,32]{2,1,0:T(1,128)}), s32[8,1,32]{2,1,0:T(1,128)S(1)}, u32[]{:S(2)}, u32[]{:S(2)}) async-start(s32[8,1,32]{2,1,0:T(1,128)} %bitcast.4), calls=%async_computation | async-start | bytes 8192 | tf_op jit(solution)/shard_map/all_to_all | solution.py:84
  36.3 114.5 %all-reduce.4.cloned.1.call-start = ((), (), s32[]{:S(2)}) async-start(), calls=%async_computation.3 | async-start | bytes 262144 | tf_op jit(solution)/shard_map/psum | solution.py:64
  68.6 8.9 %copy-start.4 = (f32[512,64]{0,1:T(8,128)S(1)}, f32[512,64]{0,1:T(8,128)}, u32[]{:S(2)}) copy-start(f32[512,64]{0,1:T(8,128)} %param.13) | copy-start | bytes 393220
  77.5 1.9 copy-start.2
  79.4 105.2 %all-reduce.6.cloned.1.call-start = ((), (), s32[]{:S(2)}) async-start(), calls=%async_computation.4 | async-start | bytes 262144 | tf_op jit(solution)/shard_map/psum | solution.py:76
  153.2 172.7 %all-reduce.8.cloned.1.call-start = ((), (), s32[]{:S(2)}) async-start(), calls=%async_computation.5 | async-start | bytes 524288 | tf_op jit(solution)/shard_map/psum | solution.py:95
  202.5 123.4 %copy-start.7 = (f32[1024]{0:T(1024)S(1)}, f32[1024]{0:T(1024)}, u32[]{:S(2)}) copy-start(f32[1024]{0:T(1024)} %param.15) | copy-start | bytes 12292
  348.7 1.4 collective-permute-start
  350.1 5.6 %copy-start.1 = (f32[512,64]{0,1:T(8,128)S(1)}, f32[512,64]{0,1:T(8,128)}, u32[]{:S(2)}) copy-start(f32[512,64]{0,1:T(8,128)} %all-reduce.6.cloned.1.call-done) | copy-start | bytes 393220
  350.1 5.6 %collective-permute-start.1 = (f32[512,64]{0,1:T(8,128)S(1)}, f32[512,64]{0,1:T(8,128)S(1)}, u32[]{:S(2)}, u32[]{:S(2)}) collective-permute-start(f32[512,64]{0,1:T(8,128)S(1)} %add.95), channel_id=1, source_target_pairs={{0,16},{8,24},{16,0},{24,8},{1,17},{9,25},{17,1},{25,9},{2,18},{10... | collective-permute-start | bytes 393224 | tf_op jit(solution)/shard_map/ppermute | solution.py:109
Sparse Core Ops, SparseCore 0:
  79.5 71.2 all-reduce.3
  153.7 30.8 all-reduce.5
  202.6 123.2 all-reduce.7
